TPU v7x, 32 devices: a whole 2x2x4 slice. The times are simulated.
32 devices in a mesh: ctx: 4 (over z), dp: 4 (over y, x), section: 2 (over core).
Axes of the slice: x: 2, y: 2, z: 4, core: 2. Of those that a mesh axis runs over, the one named last changes fastest.
Arguments:
- tokens: bfloat16 [2, 4, 512, 4096], P('section', 'dp', 'ctx'), may hold values from -6 to 6
- norm_gain: float32 [2, 4096], P('section'), may hold values from 0.1 to 1.9
- query_weight: bfloat16 [2, 4096, 512], P('section', 'dp'), may hold values from -0.421875 to 0.421875
- key_weight: bfloat16 [2, 4096, 128], P('section', 'dp'), may hold values from -0.421875 to 0.421875
- value_weight: bfloat16 [2, 4096, 128], P('section', 'dp'), may hold values from -0.09375 to 0.09375
- block_order: int32 [2, 4, 8], P('section', 'dp'), may hold values from 0 to 7, each once within a row
- doc_ids: int32 [2, 4, 512], P('section', 'dp'), may hold values from 0 to 3, never falling along the last dimension, each value on 1 to 256 neighbouring positions
Outputs:
- passed: bfloat16 [2, 4, 512, 512], P('section', 'dp', 'ctx')
Inputs may be any that keep to these rules, and one draw needn't show every extreme that they name: `block_order`: each row is a permutation of the block numbers. `doc_ids`: never falling along positions; every document holds 1 to 256 positions, and one holds exactly 256.
All inputs are finite; a program needn't handle non-finite values.
Results may differ from a plain program's by a relative error of at most 0.012.
Values may be sent and summed in bfloat16 or wider, within the bound.
No kernel may reach another device: no remote copies, remote signals or barrier semaphores. Data moves between devices by JAX's collectives and lax.ppermute only.
A program may use at most 64 MiB of HBM per device.

v0:
```python
import jax
import jax.numpy as jnp
from jax import lax
from jax.sharding import PartitionSpec as P

ROPE_BASE = 500000.0
EPSILON = 1e-05
MASKED = -1e30


def passed_along(x, axis, by):
    length = lax.axis_size(axis)
    return lax.ppermute(x, axis, [(i, (i + by) % length) for i in range(length)])


def rotate_pairs(values, positions, head_size):
    count_rows = values.shape[0]
    shaped = values.reshape(count_rows, -1, head_size)
    halfway = head_size // 2
    freqs = ROPE_BASE ** (-jnp.arange(halfway, dtype=jnp.float32) * 2.0 / head_size)
    angles = positions.astype(jnp.float32)[:, None, None] * freqs[None, None, :]
    cosine = jnp.cos(angles)
    sine = jnp.sin(angles)
    first_half = shaped[..., :halfway]
    second_half = shaped[..., halfway:]
    turned = jnp.concatenate(
        [first_half * cosine - second_half * sine, second_half * cosine + first_half * sine],
        axis=-1,
    )
    return turned.reshape(count_rows, -1)


def local(tokens, norm_gain, query_weight, key_weight, value_weight, block_order, doc_ids):
    rows_here = tokens[0, 0]
    row_count = rows_here.shape[0]
    block_rows = doc_ids.shape[2] // block_order.shape[2]
    head_size = key_weight.shape[2]
    query_width = query_weight.shape[2]
    query_heads = query_width // head_size
    widened = rows_here.astype(jnp.float32)
    normed = (
        widened
        * lax.rsqrt(jnp.mean(widened * widened, axis=-1, keepdims=True) + EPSILON)
        * norm_gain[0][None, :]
    ).astype(jnp.bfloat16)
    spread = lax.all_to_all(normed, "dp", split_axis=1, concat_axis=0, tiled=True)
    joined = jnp.concatenate([query_weight[0], key_weight[0], value_weight[0]], axis=1)
    projected = lax.psum_scatter(
        jnp.dot(spread, joined, preferred_element_type=jnp.float32),
        "dp",
        scatter_dimension=0,
        tiled=True,
    )
    q_raw = projected[:, :query_width]
    k_raw = projected[:, query_width : query_width + head_size]
    v_raw = projected[:, query_width + head_size :]
    order = block_order[0, 0]
    within = jnp.arange(block_rows, dtype=jnp.int32)
    all_positions = (order[:, None] * block_rows + within[None, :]).reshape(-1)
    key_documents = jnp.take(doc_ids[0, 0], all_positions)
    cycle_index = lax.axis_index("ctx")
    query_positions = lax.dynamic_slice_in_dim(all_positions, cycle_index * row_count, row_count)
    query_documents = lax.dynamic_slice_in_dim(key_documents, cycle_index * row_count, row_count)
    queries = (
        rotate_pairs(q_raw, query_positions, head_size)
        .astype(jnp.bfloat16)
        .reshape(row_count, query_heads, head_size)
        .transpose(1, 0, 2)
    )
    keys = rotate_pairs(k_raw, query_positions, head_size).astype(jnp.bfloat16)
    values = v_raw.astype(jnp.bfloat16)
    scaling = head_size ** (-0.5)

    def absorb(state, key_block, value_block, key_pos, key_doc):
        run_max, run_total, run_acc = state
        scores = (
            jnp.einsum("hqd,kd->hqk", queries, key_block, preferred_element_type=jnp.float32)
            * scaling
        )
        allowed = (key_doc[None, :] == query_documents[:, None]) & (
            key_pos[None, :] <= query_positions[:, None]
        )
        scores = jnp.where(allowed[None], scores, MASKED)
        new_max = jnp.maximum(run_max, jnp.max(scores, axis=-1))
        weights = jnp.where(allowed[None], jnp.exp(scores - new_max[..., None]), 0.0)
        factor = jnp.exp(run_max - new_max)
        new_total = run_total * factor + jnp.sum(weights, axis=-1)
        new_acc = run_acc * factor[..., None] + jnp.einsum(
            "hqk,kd->hqd",
            weights.astype(jnp.bfloat16),
            value_block,
            preferred_element_type=jnp.float32,
        )
        return (new_max, new_total, new_acc)

    def attend(state, pieces):
        key_piece, value_piece = pieces
        piece_rows = key_piece.shape[0]
        if piece_rows > 1024 and piece_rows % 1024 == 0:
            groups = piece_rows // 1024

            def inner(inner_state, stacked):
                return (absorb(inner_state, stacked[0], stacked[1], stacked[2], stacked[3]), None)

            stacked_all = (
                key_piece.reshape(groups, 1024, -1),
                value_piece.reshape(groups, 1024, -1),
                all_positions.reshape(groups, 1024),
                key_documents.reshape(groups, 1024),
            )
            result, unused = lax.scan(inner, state, stacked_all)
            return result
        return absorb(state, key_piece, value_piece, all_positions, key_documents)

    starting_state = (
        jnp.full((query_heads, row_count), MASKED, jnp.float32),
        jnp.zeros((query_heads, row_count), jnp.float32),
        jnp.zeros((query_heads, row_count, head_size), jnp.float32),
    )
    final_max, final_total, final_acc = attend(
        starting_state,
        (
            lax.all_gather(keys, "ctx", axis=0, tiled=True),
            lax.all_gather(values, "ctx", axis=0, tiled=True),
        ),
    )
    attended = (
        (final_acc / final_total[..., None])
        .transpose(1, 0, 2)
        .reshape(row_count, query_width)
        .astype(jnp.bfloat16)
    )
    passed = passed_along(attended, "section", 1)
    return passed[None, None]


def solution(mesh):
    in_specs = (
        P("section", "dp", "ctx", None),
        P("section", None),
        P("section", "dp", None),
        P("section", "dp", None),
        P("section", "dp", None),
        P("section", "dp", None),
        P("section", "dp", None),
    )
    out_specs = P("section", "dp", "ctx", None)
    return jax.shard_map(local, mesh=mesh, in_specs=in_specs, out_specs=out_specs, check_vma=False)
```

profile of v0, /device:TPU:0, one launch (start us, length us, event | category | flops | bytes accessed | tf_op | source)
XLA Modules:
  0.0 104.1 jit_solution(5740808734382966192)
XLA Ops:
  6.5 0.5 broadcast.241
  7.1 1.4 %reduce.4 = f32[4096]{0:T(1024)S(1)} reduce(f32[1,4096]{1,0:T(1,128)} %param.8, f32[]{:T(128)} %broadcast.241), dimensions={0}, to_apply=%param.8.reduce_sub_computation.3 | reduce | bytes 32772 | tf_op args[1]
  8.5 1.6 %copy.22 = bf16[1,1,128,4096]{2,3,1,0:T(8,128)(2,1)S(1)} copy(bf16[1,1,128,4096]{3,2,1,0:T(8,128)(2,1)} %param.7) | data formatting | bytes 2097152 | tf_op args[0]
  10.1 0.6 multiply_reduce_fusion
  10.7 0.7 multiply_convert_fusion
  11.4 19.1 %all_to_all.16 = bf16[128,4,1024]{0,2,1:T(8,128)(2,1)S(1)} all-to-all(bf16[128,4,1024]{0,2,1:T(8,128)(2,1)S(1)} %multiply_convert_fusion), channel_id=1, replica_groups=mesh['ctx'=4,'dp'=4,'section'=2] {'dp'}, dimensions={1} | all-to-all | bytes 2097152 | tf_op jit(solution)/shard_map/all_to_all | solution.py:46
  30.5 0.5 copy.23
  31.0 0.7 copy-done.1
  31.8 3.1 %fusion = f32[512,768]{0,1:T(8,128)} fusion(bf16[512,1024]{1,0:T(8,128)(2,1)S(1)} %bitcast.49, bf16[1024,128]{1,0:T(8,128)(2,1)S(1)} %bitcast.55, bf16[1024,128]{1,0:T(8,128)(2,1)} %bitcast.56, bf16[1024,512]{1,0:T(8,128)(2,1)S(1)} %bitcast.54), kind=kOutput, calls=%fused_computation.3 | convolution fusion | flops 810024960 | bytes 4194304 | tf_op jit(solution)/shard_map/dot_general | solution.py:49
  34.9 0.6 copy-done.3
  35.8 3.5 %gather_fusion = s32[512]{0:T(512)S(1)} fusion(s32[512]{0:T(512)S(1)} %bitcast.46, s32[1024]{0:T(1024)S(1)} %pad_clamp_fusion), kind=kCustom, calls=%fused_computation | custom fusion | bytes 6144 | tf_op jit(solution)/shard_map/jit(_take)/gather | solution.py:60
  39.6 0.3 multiply_cosine_fusion
  40.0 26.0 %reduce-scatter.2.cloned.1.call-done = f32[128,768]{0,1:T(8,128)} async-done(((f32[512,768]{0,1:T(8,128)}), f32[128,768]{0,1:T(8,128)}) %reduce-scatter.2.cloned.1.call-update) | async-done | bytes 393232 | tf_op jit(solution)/shard_map/reduce_scatter | solution.py:48
  65.9 0.8 slice_bitcast_fusion
  66.8 0.2 fusion.25
  67.0 12.3 %all-gather = bf16[512,1,128]{0,2,1:T(8,128)(2,1)S(1)} all-gather(bf16[128,1,128]{0,2,1:T(8,128)(2,1)S(1)} %pad_maximum_fusion), channel_id=2, replica_groups=mesh['ctx'=4,'dp'=4,'section'=2] {'ctx'}, dimensions={0}, use_global_device_ids=true | all-gather | bytes 163840 | tf_op jit(solution)/shard_map/all_gather | solution.py:123
  79.3 1.0 slice.31
  80.7 0.5 fusion.33
  81.1 0.9 slice.44
  82.0 12.2 %all_gather.7 = bf16[512,128]{0,1:T(8,128)(2,1)S(1)} all-gather(bf16[128,128]{0,1:T(8,128)(2,1)S(1)} %slice.44), channel_id=1, replica_groups=mesh['ctx'=4,'dp'=4,'section'=2] {'ctx'}, dimensions={0}, use_global_device_ids=true | all-gather | bytes 163840 | tf_op jit(solution)/shard_map/all_gather | solution.py:124
  94.2 0.3 fusion.10
  94.6 0.5 fusion.9
  95.3 1.3 %collective-permute-done = bf16[128,512]{1,0:T(8,128)(2,1)S(1)} collective-permute-done((bf16[128,512]{1,0:T(8,128)(2,1)S(1)}, bf16[128,512]{1,0:T(8,128)(2,1)S(1)}, u32[]{:S(2)}, u32[]{:S(2)}) %collective-permute-start) | collective-permute-done | bytes 131104 | tf_op jit(solution)/shard_map/ppermute | solution.py:13
  96.6 0.7 copy.35
  (30 shorter events, 1.2 us)
Async XLA Ops:
  6.5 29.3 %copy-start = (s32[1,1,512]{2,1,0:T(1,128)S(1)}, s32[1,1,512]{2,1,0:T(1,128)}, u32[]{:S(2)}) copy-start(s32[1,1,512]{2,1,0:T(1,128)} %param.13) | copy-start | bytes 6148
  6.5 59.4 %reduce-scatter.2.cloned.1.call-start = ((), (), s32[]{:S(2)}) async-start(), calls=%async_computation.2 | async-start | bytes 1966080 | tf_op jit(solution)/shard_map/reduce_scatter | solution.py:48
  30.5 1.2 %copy-start.1 = (bf16[1,1024,512]{2,1,0:T(8,128)(2,1)S(1)}, bf16[1,1024,512]{2,1,0:T(8,128)(2,1)}, u32[]{:S(2)}) copy-start(bf16[1,1024,512]{2,1,0:T(8,128)(2,1)} %param.9) | copy-start | bytes 3145732
  30.5 1.3 %copy-start.2 = (bf16[1,1024,128]{2,1,0:T(8,128)(2,1)S(1)}, bf16[1,1024,128]{2,1,0:T(8,128)(2,1)}, u32[]{:S(2)}) copy-start(bf16[1,1024,128]{2,1,0:T(8,128)(2,1)} %param.11) | copy-start | bytes 786436
  34.9 0.7 copy-start.3
  95.2 1.4 %collective-permute-start = (bf16[128,512]{1,0:T(8,128)(2,1)S(1)}, bf16[128,512]{1,0:T(8,128)(2,1)S(1)}, u32[]{:S(2)}, u32[]{:S(2)}) collective-permute-start(bf16[128,512]{1,0:T(8,128)(2,1)S(1)} %copy.28), channel_id=1, source_target_pairs={{0,1},{1,0},{2,3},{3,2},{4,5},{5,4},{6,7},{7,6},{8,9},{9,8},{10,11... | collective-permute-start | bytes 393224 | tf_op jit(solution)/shard_map/ppermute | solution.py:13
Sparse Core Ops, SparseCore 0:
  35.0 30.8 reduce-scatter.1
where the time goes:
time: 105 us; the launch traced here: 104 us
  blocking collectives  43.7 us (42%)
  waiting for transfers between devices  27.3 us (26%)
  between operations  13.5 us (13%)
  local copies, waits for them, and re-layouts  11.5 us (11%)
  matrix products  4.04 us (4%)
  other arithmetic  3.93 us (4%)
    reduce_scatter x1, waiting for transfers between devices, local(): lax.psum_scatter(jnp.dot(spread, joined, preferred_element_type=jnp.float...  26 us
    all_to_all x1, blocking collectives, local(): lax.all_to_all(normed, 'dp', split_axis=1, concat_axis=0, tiled=True)  19.1 us
    all_gather x1, blocking collectives, local(): lax.all_gather(keys, 'ctx', axis=0, tiled=True)  12.3 us
    all_gather x1, blocking collectives, local(): lax.all_gather(values, 'ctx', axis=0, tiled=True)  12.2 us
    unnamed x13, local copies, waits for them, and re-layouts  4.4 us
    gather x1, local copies, waits for them, and re-layouts, local(): key_documents = jnp.take(doc_ids[0, 0], all_positions)  3.51 us
    dot_general x1, matrix products, local(): jnp.dot(spread, joined, preferred_element_type=jnp.float32)  3.13 us
  transfers between devices with their start and end apart: 2, of which 2 were waited for; matrix products, arithmetic and copies ran while one was open for 4% of the time, Pallas kernels for 0%

commit v1 on v0

--- a/solution.py
+++ b/solution.py
@@ -31,6 +31,17 @@
 
 
 def local(tokens, norm_gain, query_weight, key_weight, value_weight, block_order, doc_ids):
+
+    def obtain_side(x_part, net_axis):
+        finding = jax.lax.all_to_all(
+            jnp.concatenate(tuple((x_part for _ in range(jax.lax.axis_size(net_axis)))), axis=0),
+            net_axis,
+            0,
+            0,
+            tiled=True,
+        )
+        return finding
+
     rows_here = tokens[0, 0]
     row_count = rows_here.shape[0]
     block_rows = doc_ids.shape[2] // block_order.shape[2]
@@ -119,10 +130,7 @@
     )
     final_max, final_total, final_acc = attend(
         starting_state,
-        (
-            lax.all_gather(keys, "ctx", axis=0, tiled=True),
-            lax.all_gather(values, "ctx", axis=0, tiled=True),
-        ),
+        (lax.all_gather(keys, "ctx", axis=0, tiled=True), obtain_side(values, "ctx")),
     )
     attended = (
         (final_acc / final_total[..., None])

time: 105 us -> 97.3 us (0.927)
  blocking collectives: 43.7 us -> 32 us
  starting transfers between devices: 0.07 us -> 4.66 us
    all_gather x1 -> x0, blocking collectives: 12.2 us -> none  [local(): lax.all_gather(values, 'ctx', axis=0, tiled=True)]
    all_to_all x0 -> x1, starting transfers between devices: none -> 4.59 us  [obtain_side(): jax.lax.all_to_all(jnp.concatenate(tuple((x_part for _ in range(jax.lax.a...]
  transfers between devices with their start and end apart: 2 -> 3, of which waited for: 2 -> 2; matrix products, arithmetic and copies ran while one was open for 4% -> 7% of each run, Pallas kernels for 0% -> 0%
where the time goes in v1:
time: 97.3 us; the launch traced here: 96.9 us
  blocking collectives  32 us (33%)
  waiting for transfers between devices  27.3 us (28%)
  between operations  13.6 us (14%)
  local copies, waits for them, and re-layouts  10.7 us (11%)
  starting transfers between devices  4.66 us (5%)
  other arithmetic  4.61 us (5%)
  matrix products  4.04 us (4%)
    reduce_scatter x1, waiting for transfers between devices, local(): lax.psum_scatter(jnp.dot(spread, joined, preferred_element_type=jnp.float...  26 us
    all_to_all x1, blocking collectives, local(): lax.all_to_all(normed, 'dp', split_axis=1, concat_axis=0, tiled=True)  19.1 us
    all_gather x1, blocking collectives, local(): lax.all_gather(keys, 'ctx', axis=0, tiled=True)  12.8 us
    all_to_all x1, starting transfers between devices, obtain_side(): jax.lax.all_to_all(jnp.concatenate(tuple((x_part for _ in range(jax.lax.a...  4.59 us
    unnamed x13, local copies, waits for them, and re-layouts  4.4 us
    gather x1, local copies, waits for them, and re-layouts, local(): key_documents = jnp.take(doc_ids[0, 0], all_positions)  3.51 us
    dot_general x1, matrix products, local(): jnp.dot(spread, joined, preferred_element_type=jnp.float32)  3.14 us
  transfers between devices with their start and end apart: 3, of which 2 were waited for; matrix products, arithmetic and copies ran while one was open for 7% of the time, Pallas kernels for 0%

profile of v1, /device:TPU:0, one launch (start us, length us, event | category | flops | bytes accessed | tf_op | source)
XLA Modules:
  0.0 96.9 jit_solution(7422109725364633413)
XLA Ops:
  6.5 0.5 broadcast.241
  7.1 1.4 %reduce.4 = f32[4096]{0:T(1024)S(1)} reduce(f32[1,4096]{1,0:T(1,128)} %param.8, f32[]{:T(128)} %broadcast.241), dimensions={0}, to_apply=%param.8.reduce_sub_computation.3 | reduce | bytes 32772 | tf_op args[1]
  8.5 1.6 %copy.29 = bf16[1,1,128,4096]{2,3,1,0:T(8,128)(2,1)S(1)} copy(bf16[1,1,128,4096]{3,2,1,0:T(8,128)(2,1)} %param.7) | data formatting | bytes 2097152 | tf_op args[0]
  10.1 0.6 multiply_reduce_fusion
  10.7 0.7 multiply_convert_fusion
  11.4 19.1 %all_to_all.28 = bf16[128,4,1024]{0,2,1:T(8,128)(2,1)S(1)} all-to-all(bf16[128,4,1024]{0,2,1:T(8,128)(2,1)S(1)} %multiply_convert_fusion), channel_id=1, replica_groups=mesh['ctx'=4,'dp'=4,'section'=2] {'dp'}, dimensions={1} | all-to-all | bytes 2097152 | tf_op jit(solution)/shard_map/all_to_all | solution.py:57
  30.5 0.5 copy.30
  31.0 0.7 copy-done.1
  31.8 3.1 %fusion = f32[512,768]{0,1:T(8,128)} fusion(bf16[512,1024]{1,0:T(8,128)(2,1)S(1)} %bitcast.54, bf16[1024,128]{1,0:T(8,128)(2,1)S(1)} %bitcast.60, bf16[1024,128]{1,0:T(8,128)(2,1)} %bitcast.61, bf16[1024,512]{1,0:T(8,128)(2,1)S(1)} %bitcast.59), kind=kOutput, calls=%fused_computation.3 | convolution fusion | flops 810024960 | bytes 4194304 | tf_op jit(solution)/shard_map/dot_general | solution.py:60
  34.9 0.6 copy-done.3
  35.8 3.5 %gather_fusion = s32[512]{0:T(512)S(1)} fusion(s32[512]{0:T(512)S(1)} %bitcast.51, s32[1024]{0:T(1024)S(1)} %pad_clamp_fusion), kind=kCustom, calls=%fused_computation | custom fusion | bytes 6144 | tf_op jit(solution)/shard_map/jit(_take)/gather | solution.py:71
  39.7 0.3 multiply_cosine_fusion
  40.0 26.0 %reduce-scatter.2.cloned.1.call-done = f32[128,768]{0,1:T(8,128)} async-done(((f32[512,768]{0,1:T(8,128)}), f32[128,768]{0,1:T(8,128)}) %reduce-scatter.2.cloned.1.call-update) | async-done | bytes 393232 | tf_op jit(solution)/shard_map/reduce_scatter | solution.py:59
  65.9 0.9 slice.44
  66.8 0.7 copy_bitcast_fusion
  67.5 4.6 %all-to-all-start.1 = ((bf16[4,128,128]{1,2,0:T(8,128)(2,1)}), bf16[4,128,128]{1,2,0:T(8,128)(2,1)S(1)}, u32[]{:S(2)}, u32[]{:S(2)}) async-start(bf16[4,128,128]{1,2,0:T(8,128)(2,1)} %copy_bitcast_fusion), calls=%async_computation.2 | async-start | bytes 262144 | tf_op jit(solution)/shard_map/all_to_all | solution.py:36
  72.1 0.8 slice_bitcast_fusion
  72.9 0.2 fusion.24
  73.2 12.8 %all-gather = bf16[512,1,128]{0,2,1:T(8,128)(2,1)S(1)} all-gather(bf16[128,1,128]{0,2,1:T(8,128)(2,1)S(1)} %pad_maximum_fusion), channel_id=2, replica_groups=mesh['ctx'=4,'dp'=4,'section'=2] {'ctx'}, dimensions={0}, use_global_device_ids=true | all-gather | bytes 163840 | tf_op jit(solution)/shard_map/all_gather | solution.py:133
  86.4 0.5 fusion.32
  86.8 0.4 fusion.10
  87.4 0.5 fusion.9
  88.0 1.3 %collective-permute-done = bf16[128,512]{1,0:T(8,128)(2,1)S(1)} collective-permute-done((bf16[128,512]{1,0:T(8,128)(2,1)S(1)}, bf16[128,512]{1,0:T(8,128)(2,1)S(1)}, u32[]{:S(2)}, u32[]{:S(2)}) %collective-permute-start) | collective-permute-done | bytes 131104 | tf_op jit(solution)/shard_map/ppermute | solution.py:13
  89.4 0.7 copy.46
  (35 shorter events, 1.4 us)
Async XLA Ops:
  6.5 29.3 %copy-start = (s32[1,1,512]{2,1,0:T(1,128)S(1)}, s32[1,1,512]{2,1,0:T(1,128)}, u32[]{:S(2)}) copy-start(s32[1,1,512]{2,1,0:T(1,128)} %param.13) | copy-start | bytes 6148
  6.5 59.4 %reduce-scatter.2.cloned.1.call-start = ((), (), s32[]{:S(2)}) async-start(), calls=%async_computation.3 | async-start | bytes 1966080 | tf_op jit(solution)/shard_map/reduce_scatter | solution.py:59
  30.5 1.2 %copy-start.1 = (bf16[1,1024,512]{2,1,0:T(8,128)(2,1)S(1)}, bf16[1,1024,512]{2,1,0:T(8,128)(2,1)}, u32[]{:S(2)}) copy-start(bf16[1,1024,512]{2,1,0:T(8,128)(2,1)} %param.9) | copy-start | bytes 3145732
  30.5 1.3 %copy-start.2 = (bf16[1,1024,128]{2,1,0:T(8,128)(2,1)S(1)}, bf16[1,1024,128]{2,1,0:T(8,128)(2,1)}, u32[]{:S(2)}) copy-start(bf16[1,1024,128]{2,1,0:T(8,128)(2,1)} %param.11) | copy-start | bytes 786436
  34.9 0.7 copy-start.3
  65.9 20.0 %slice-start = ((f32[128,768]{0,1:T(8,128)}), f32[128,512]{0,1:T(8,128)S(1)}, s32[]{:S(2)}) async-start(f32[128,768]{0,1:T(8,128)} %reduce-scatter.2.cloned.1.call-done), calls=%async_computation.4 | async-start | bytes 524288 | tf_op jit(solution)/shard_map/slice | solution.py:65
  67.5 19.7 %all-to-all-start.1 = ((bf16[4,128,128]{1,2,0:T(8,128)(2,1)}), bf16[4,128,128]{1,2,0:T(8,128)(2,1)S(1)}, u32[]{:S(2)}, u32[]{:S(2)}) async-start(bf16[4,128,128]{1,2,0:T(8,128)(2,1)} %copy_bitcast_fusion), calls=%async_computation.2 | async-start | bytes 262144 | tf_op jit(solution)/shard_map/all_to_all | solution.py:36
  88.0 1.4 %collective-permute-start = (bf16[128,512]{1,0:T(8,128)(2,1)S(1)}, bf16[128,512]{1,0:T(8,128)(2,1)S(1)}, u32[]{:S(2)}, u32[]{:S(2)}) collective-permute-start(bf16[128,512]{1,0:T(8,128)(2,1)S(1)} %copy.37), channel_id=1, source_target_pairs={{0,1},{1,0},{2,3},{3,2},{4,5},{5,4},{6,7},{7,6},{8,9},{9,8},{10,11... | collective-permute-start | bytes 393224 | tf_op jit(solution)/shard_map/ppermute | solution.py:13
Sparse Core Ops, SparseCore 0:
  35.1 30.8 reduce-scatter.1
